TPU v7x, 32 devices: a whole 2x2x4 slice. The times are simulated.
32 devices in a mesh: tile: 4 (over y, x), atom: 8 (over z, core).
Axes of the slice: x: 2, y: 2, z: 4, core: 2. Of those that a mesh axis runs over, the one named last changes fastest.
Arguments:
- image: bfloat16 [64, 32, 512], P(None, 'tile'), may hold values from -10 to 10
- coeffs: bfloat16 [512, 32, 512], P('atom', 'tile'), may hold values from -5 to 5
- dictionary: bfloat16 [512, 5184], P('atom'), may hold values from -0.078125 to 0.078125
- shrink: float32 [512], P('atom'), may hold values from 0.05 to 0.5
- seam_map: int32 [4, 512], replicated, may hold values from 0 to 1
Outputs:
- new_coeffs: bfloat16 [512, 32, 512], P('atom', 'tile')
- residual: bfloat16 [64, 32, 512], P(None, 'tile')
- atom_step: float32 [512, 5184], P('atom', 'tile')
All inputs are finite; a program needn't handle non-finite values.
Results may differ from a plain program's by a relative error of at most 0.0029.
Values may be sent and summed in bfloat16 or wider, within the bound.
A program may use at most 64 MiB of HBM per device.

v0:
```python
import jax
import jax.numpy as jnp
from jax import lax
from jax.sharding import PartitionSpec as P

TAP = 9
RIM = TAP // 2
BLOCK = 4
SPAN = BLOCK + TAP - 1

step_size = 0.1
eps_sq = 0.01


def rims(block):
    count = lax.axis_size("tile")
    forward = [(i, (i + 1) % count) for i in range(count)]
    backward = [(target, source) for source, target in forward]
    low = lax.ppermute(block[-RIM:], "tile", forward)
    high = lax.ppermute(block[:RIM], "tile", backward)
    return low, high


def columns(padded, width):
    wide = jnp.pad(padded, ((0, 0), (0, 0), (RIM, RIM)))
    return jnp.stack([wide[:, :, d : d + width] for d in range(TAP)], axis=1)


def banded(taps):
    parts = [
        jnp.pad(taps, ((j, BLOCK - 1 - j), (0, 0), (0, 0), (0, 0))) for j in range(BLOCK)
    ]
    return jnp.concatenate(parts, axis=3).reshape(SPAN * TAP * taps.shape[2], -1)


def windows(cols, rows):
    for start in range(0, rows, BLOCK):
        part = cols[start : start + SPAN]
        yield start, part.reshape(-1, part.shape[-1])


def apply_band(cols, band, rows):
    outs = []
    for _, window in windows(cols, rows):
        outs.append(
            lax.dot_general(
                band, window, (((0,), (0,)), ((), ())), preferred_element_type=jnp.float32
            )
        )
    return jnp.concatenate(outs, axis=0).reshape(rows, -1, cols.shape[-1])


def per_device(image, coeffs, dictionary, shrink, seam_map):
    local_atoms, strip_rows, width = coeffs.shape
    chans = image.shape[0]
    strips = lax.axis_size("tile")
    position = lax.axis_index("tile")
    seam_float = seam_map.astype(jnp.float32)
    w_down = (0.5 + 0.5 * seam_float[position]).astype(jnp.bfloat16)
    w_up = (0.5 + 0.5 * seam_float[(position + strips - 1) % strips]).astype(jnp.bfloat16)

    own = coeffs.transpose(1, 0, 2)
    low, high = rims(own)
    coef_cols = columns(jnp.concatenate([low * w_up, own, high * w_down], axis=0), width)
    taps = dictionary.reshape(local_atoms, chans, TAP, TAP).transpose(2, 3, 0, 1)
    partial_value = apply_band(coef_cols, banded(taps), strip_rows)
    share = lax.psum_scatter(partial_value, "atom", scatter_dimension=1, tiled=True)
    band_count = share.shape[1]
    own_bands = lax.dynamic_slice_in_dim(image, lax.axis_index("atom") * band_count, band_count, 0)
    resid_share = (own_bands.transpose(1, 0, 2).astype(jnp.float32) - share).astype(jnp.bfloat16)
    low, high = rims(resid_share)
    share_padded = jnp.concatenate([low * w_up, resid_share, high * w_down], axis=0)
    resid_padded = lax.all_gather(share_padded, "atom", axis=1, tiled=True)
    residual = resid_padded[RIM : RIM + strip_rows].transpose(1, 0, 2)
    resid_cols = columns(resid_padded, width)
    flipped = taps[::-1, ::-1].transpose(0, 1, 3, 2)

    terms = 0.0
    for start, window in windows(resid_cols, strip_rows):
        rows = own[start : start + BLOCK].reshape(BLOCK * local_atoms, width)
        terms += lax.dot_general(
            window, rows, (((1,), (1,)), ((), ())), preferred_element_type=jnp.float32
        )
    terms = terms.reshape(SPAN, TAP, chans, BLOCK * local_atoms)
    summed = sum(
        terms[j : j + TAP, :, :, j * local_atoms : (j + 1) * local_atoms] for j in range(BLOCK)
    )
    scale = 1.0 / jnp.sqrt(jnp.float32(strip_rows * strips * width))
    part = lax.psum_scatter(summed * scale, "tile", scatter_dimension=2, tiled=True)
    atom_step = part[::-1, ::-1].transpose(3, 2, 0, 1).reshape(local_atoms, -1)

    correlation = apply_band(resid_cols, banded(flipped), strip_rows).transpose(1, 0, 2)
    updated = coeffs.astype(jnp.float32) + step_size * correlation
    new_coeffs = (
        updated - shrink[:, None, None] * updated / jnp.sqrt(updated * updated + eps_sq)
    ).astype(jnp.bfloat16)
    return (new_coeffs, residual, atom_step)


def solution(mesh):
    placed = (P(None, "tile", None), P("atom", "tile", None), P("atom", None), P("atom"), P())
    return jax.shard_map(
        per_device,
        mesh=mesh,
        in_specs=placed,
        out_specs=(P("atom", "tile", None), P(None, "tile", None), P("atom", "tile")),
        check_vma=False,
    )
```

profile of v0, /device:TPU:9, one launch (start us, length us, event | category | flops | bytes accessed | tf_op | source)
XLA Modules:
  0.0 212.0 jit_solution(10860286660782709906)
XLA Ops:
  7.2 1.2 copy.86
  12.4 2.4 %copy.31 = bf16[64,5184]{0,1:T(8,128)(2,1)} copy(bf16[64,5184]{1,0:T(8,128)(2,1)} %param.7) | data formatting | bytes 1327104 | tf_op args[2]
  14.8 2.6 %reshape.64 = bf16[64,64,9,9]{0,3,2,1:T(8,128)(2,1)S(1)} reshape(bf16[64,5184]{0,1:T(8,128)(2,1)} %copy.31) | data formatting | bytes 1327104 | tf_op jit(solution)/shard_map/reshape | solution.py:65
  17.4 2.5 %copy.32 = bf16[64,64,9,9]{1,0,3,2:T(8,128)(2,1)} copy(bf16[64,64,9,9]{0,3,2,1:T(8,128)(2,1)S(1)} %reshape.64) | data formatting | bytes 1327104 | tf_op jit(solution)/shard_map/reshape | solution.py:65
  20.8 2.5 %collective-permute-done.1 = bf16[4,64,512]{2,1,0:T(8,128)(2,1)} collective-permute-done((bf16[4,64,512]{2,1,0:T(8,128)(2,1)}, bf16[4,64,512]{2,1,0:T(8,128)(2,1)}, u32[]{:S(2)}, u32[]{:S(2)}) %collective-permute-start.1) | collective-permute-done | bytes 262176 | tf_op jit(solution)/shard_map/ppermute | solution.py:20
  28.6 3.0 %fusion.26 = f32[256,512]{1,0:T(8,128)S(1)} fusion(bf16[16,9,64,512]{3,2,1,0:T(8,128)(2,1)S(1)} %fusion.44, bf16[9,9,64,64]{3,2,1,0:T(8,128)(2,1)S(1)} %bitcast.154), kind=kOutput, calls=%fused_computation.43 | convolution fusion | flops 1847328768 | bytes 8929280 | tf_op jit(solution)/shard_map/dot_general | solution.py:46
  31.6 3.0 %fusion.23 = f32[256,512]{1,0:T(8,128)S(1)} fusion(bf16[16,9,64,512]{3,2,1,0:T(8,128)(2,1)S(1)} %fusion.44, bf16[9,9,64,64]{3,2,1,0:T(8,128)(2,1)S(1)} %bitcast.155), kind=kOutput, calls=%fused_computation.42 | convolution fusion | flops 1847328768 | bytes 8929280 | tf_op jit(solution)/shard_map/dot_general | solution.py:46
  35.7 27.1 %reduce-scatter.3.cloned.1.call-done = f32[8,8,512]{2,1,0:T(8,128)} async-done(((f32[8,64,512]{2,1,0:T(8,128)}), f32[8,8,512]{2,1,0:T(8,128)}) %reduce-scatter.3.cloned.1.call-update) | async-done | bytes 131088 | tf_op jit(solution)/shard_map/reduce_scatter | solution.py:67
  63.8 1.3 collective-permute-start.2
  66.2 1.3 collective-permute-done.2
  69.3 28.4 %all-gather.2.cloned.1.call-done = bf16[16,64,512]{2,1,0:T(8,128)(2,1)} async-done(((bf16[16,8,512]{2,1,0:T(8,128)(2,1)}), bf16[16,64,512]{2,1,0:T(8,128)(2,1)}) %all-gather.2.cloned.1.call-update) | async-done | bytes 1048592 | tf_op jit(solution)/shard_map/all_gather | solution.py:73
  99.9 1.6 fusion.46
  101.5 1.7 fusion.48
  103.3 1.7 fusion.50
  107.6 4.6 %fusion.68 = (bf16[12,9,64,512]{3,2,1,0:T(8,128)(2,1)}, bf16[12,9,64,512]{3,2,1,0:T(8,128)(2,1)S(1)}) fusion(bf16[16,9,64,512]{3,2,1,0:T(8,128)(2,1)S(1)} %fusion.60), kind=kLoop, calls=%fused_computation.113 | loop fusion | bytes 28311552 | tf_op jit(solution)/shard_map/slice | solution.py:38
  113.4 3.0 %convolution_bitcast_fusion = f32[256,512]{1,0:T(8,128)} fusion(bf16[16,9,64,512]{3,2,1,0:T(8,128)(2,1)S(1)} %fusion.60, bf16[9,9,64,64]{2,3,1,0:T(8,128)(2,1)S(1)} %reverse_bitcast_fusion), kind=kOutput, calls=%fused_computation.40 | convolution fusion | flops 1847328768 | bytes 8929280 | tf_op jit(solution)/shard_map/dot_general | solution.py:46
  116.3 3.0 %fusion.72 = f32[6912,256]{1,0:T(8,128)S(1)} fusion(bf16[6912,512]{1,0:T(8,128)(2,1)S(1)} %bitcast.149, bf16[256,512]{1,0:T(8,128)(2,1)} %bitcast.51), kind=kOutput, calls=%fused_computation.117 | convolution fusion | flops 1811939328 | bytes 14417920 | tf_op jit(solution)/shard_map/dot_general | solution.py:81
  119.3 5.0 %convolution_add_fusion = f32[6912,256]{1,0:T(8,128)S(1)} fusion(f32[6912,256]{1,0:T(8,128)S(1)} %fusion.72, bf16[6912,512]{1,0:T(8,128)(2,1)} %bitcast.150, bf16[256,512]{1,0:T(8,128)(2,1)} %bitcast.53), kind=kOutput, calls=%fused_computation.16 | convolution fusion | flops 1813708800 | bytes 21495808 | tf_op jit(solution)/shard_map/dot_general | solution.py:81
  124.4 4.4 %fusion.69 = (f32[9,9,64,64]{3,2,1,0:T(8,128)S(1)}, f32[9,9,64,64]{3,2,1,0:T(8,128)S(1)}, f32[9,9,64,64]{3,2,1,0:T(8,128)}, f32[9,9,64,64]{3,2,1,0:T(8,128)}) fusion(f32[12,9,64,256]{3,2,1,0:T(8,128)S(1)} %bitcast.148), kind=kLoop, calls=%fused_computation.114 | loop fusion | bytes 10616832 | tf_op jit(solution)/shard_map/slice | solution.py:86
  128.8 17.3 %fusion.19 = f32[9,9,64,64]{3,1,0,2:T(8,128)} fusion(f32[9,9,64,64]{3,2,1,0:T(8,128)} %get-tuple-element.16, f32[9,9,64,64]{3,2,1,0:T(8,128)S(1)} %get-tuple-element.14, f32[9,9,64,64]{3,2,1,0:T(8,128)} %get-tuple-element.15, f32[9,9,64,64]{3,2,1,0:T(8,128)S(1)} %get-tuple-element.13), kind=kLoop, calls=%fused_computation.33 | loop fusion | flops 1327104 | bytes 6635520 | tf_op jit(solution)/shard_map/mul | solution.py:89
  146.2 8.1 %convolution_bitcast_fusion.1 = f32[256,512]{1,0:T(8,128)S(1)} fusion(bf16[16,9,64,512]{3,2,1,0:T(8,128)(2,1)} %copy-done.3, bf16[9,9,64,64]{2,3,1,0:T(8,128)(2,1)S(1)} %reverse_bitcast_fusion), kind=kOutput, calls=%fused_computation.41 | convolution fusion | flops 1847328768 | bytes 8265728 | tf_op jit(solution)/shard_map/dot_general | solution.py:46
  154.5 1.5 subtract_convert_fusion
  155.9 46.2 %reduce-scatter.5.cloned.1.call-done = f32[9,9,16,64]{3,1,0,2:T(8,128)} async-done(((f32[9,9,64,64]{3,1,0,2:T(8,128)}), f32[9,9,16,64]{3,1,0,2:T(8,128)}) %reduce-scatter.5.cloned.1.call-update) | async-done | bytes 331792 | tf_op jit(solution)/shard_map/reduce_scatter | solution.py:89
  202.2 2.2 %rev.7 = f32[9,9,16,64]{3,1,0,2:T(8,128)S(1)} reverse(f32[9,9,16,64]{3,1,0,2:T(8,128)} %reduce-scatter.5.cloned.1.call-done), dimensions={0,1} | reverse | bytes 663552 | tf_op jit(solution)/shard_map/rev | solution.py:90
  (61 shorter events, 22.0 us)
Async XLA Ops:
  7.2 28.6 %copy-start = (bf16[64,8,512]{2,1,0:T(8,128)(2,1)S(1)}, bf16[64,8,512]{2,1,0:T(8,128)(2,1)}, u32[]{:S(2)}) copy-start(bf16[64,8,512]{2,1,0:T(8,128)(2,1)} %param.5) | copy-start | bytes 1572868
  7.2 55.7 %reduce-scatter.3.cloned.1.call-start = ((), (), s32[]{:S(2)}) async-start(), calls=%async_computation.2 | async-start | bytes 1179648 | tf_op jit(solution)/shard_map/reduce_scatter | solution.py:67
  9.3 10.5 %collective-permute-start = (bf16[4,64,512]{2,1,0:T(8,128)(2,1)}, bf16[4,64,512]{2,1,0:T(8,128)(2,1)}, u32[]{:S(2)}, u32[]{:S(2)}) collective-permute-start(bf16[4,64,512]{2,1,0:T(8,128)(2,1)} %get-tuple-element.17), channel_id=1, source_target_pairs={{0,8},{8,16},{16,24},{24,0},{1,9},{9,17},{17,25},{25,1},{2,10},{10... | collective-permute-start | bytes 786440 | tf_op jit(solution)/shard_map/ppermute | solution.py:19
  10.5 12.9 %collective-permute-start.1 = (bf16[4,64,512]{2,1,0:T(8,128)(2,1)}, bf16[4,64,512]{2,1,0:T(8,128)(2,1)}, u32[]{:S(2)}, u32[]{:S(2)}) collective-permute-start(bf16[4,64,512]{2,1,0:T(8,128)(2,1)} %get-tuple-element.18), channel_id=1, source_target_pairs={{8,0},{16,8},{24,16},{0,24},{9,1},{17,9},{25,17},{1,25},{10,2},{18... | collective-permute-start | bytes 786440 | tf_op jit(solution)/shard_map/ppermute | solution.py:20
  25.5 3.1 %copy-start.4 = (bf16[64,64,9,9]{1,0,3,2:T(8,128)(2,1)S(1)}, bf16[64,64,9,9]{1,0,3,2:T(8,128)(2,1)}, u32[]{:S(2)}) copy-start(bf16[64,64,9,9]{1,0,3,2:T(8,128)(2,1)} %copy.32) | copy-start | bytes 1990660
  35.7 62.0 %all-gather.2.cloned.1.call-start = ((), (), s32[]{:S(2)}) async-start(), calls=%async_computation.3 | async-start | bytes 1179648 | tf_op jit(solution)/shard_map/all_gather | solution.py:73
  63.8 3.7 %collective-permute-start.2 = (bf16[4,8,512]{2,1,0:T(8,128)(2,1)S(1)}, bf16[4,8,512]{2,1,0:T(8,128)(2,1)S(1)}, u32[]{:S(2)}, u32[]{:S(2)}) collective-permute-start(bf16[4,8,512]{2,1,0:T(8,128)(2,1)S(1)} %get-tuple-element.19), channel_id=1, source_target_pairs={{0,8},{8,16},{16,24},{24,0},{1,9},{9,17},{17,25},{25,1},{2,10},{10... | collective-permute-start | bytes 98312 | tf_op jit(solution)/shard_map/ppermute | solution.py:19
  65.2 3.1 %collective-permute-start.3 = (bf16[4,8,512]{2,1,0:T(8,128)(2,1)S(1)}, bf16[4,8,512]{2,1,0:T(8,128)(2,1)S(1)}, u32[]{:S(2)}, u32[]{:S(2)}) collective-permute-start(bf16[4,8,512]{2,1,0:T(8,128)(2,1)S(1)} %get-tuple-element.20), channel_id=1, source_target_pairs={{8,0},{16,8},{24,16},{0,24},{9,1},{17,9},{25,17},{1,25},{10,2},{18... | collective-permute-start | bytes 98312 | tf_op jit(solution)/shard_map/ppermute | solution.py:20
  68.9 133.2 %reduce-scatter.5.cloned.1.call-start = ((), (), s32[]{:S(2)}) async-start(), calls=%async_computation.4 | async-start | bytes 5898240 | tf_op jit(solution)/shard_map/reduce_scatter | solution.py:89
  97.6 7.4 %copy-start.2 = (bf16[16,64,512]{2,1,0:T(8,128)(2,1)S(1)}, bf16[16,64,512]{2,1,0:T(8,128)(2,1)}, u32[]{:S(2)}) copy-start(bf16[16,64,512]{2,1,0:T(8,128)(2,1)} %all-gather.2.cloned.1.call-done) | copy-start | bytes 3145732
  107.6 5.8 %copy-start.3 = (bf16[16,9,64,512]{3,2,1,0:T(8,128)(2,1)}, bf16[16,9,64,512]{3,2,1,0:T(8,128)(2,1)S(1)}, u32[]{:S(2)}) copy-start(bf16[16,9,64,512]{3,2,1,0:T(8,128)(2,1)S(1)} %fusion.60) | copy-start | bytes 28311556
  146.1 8.2 %copy-start.6 = (f32[256,512]{1,0:T(8,128)S(1)}, f32[256,512]{1,0:T(8,128)}, u32[]{:S(2)}) copy-start(f32[256,512]{1,0:T(8,128)} %convolution_bitcast_fusion) | copy-start | bytes 1572868
  146.1 8.3 %copy-start.5 = (bf16[64,8,512]{2,1,0:T(8,128)(2,1)S(1)}, bf16[64,8,512]{2,1,0:T(8,128)(2,1)}, u32[]{:S(2)}) copy-start(bf16[64,8,512]{2,1,0:T(8,128)(2,1)} %param.6) | copy-start | bytes 1572868
  146.1 8.3 %copy-start.7 = (f32[64]{0:T(128)S(1)}, f32[64]{0:T(128)}, u32[]{:S(2)}) copy-start(f32[64]{0:T(128)} %param.8) | copy-start | bytes 772
  146.1 59.3 %copy-start.1 = (bf16[64,8,512]{2,1,0:T(8,128)(2,1)S(1)}, bf16[64,8,512]{2,1,0:T(8,128)(2,1)}, u32[]{:S(2)}) copy-start(bf16[64,8,512]{2,1,0:T(8,128)(2,1)} %param.5) | copy-start | bytes 1572868
Sparse Core Ops, SparseCore 0:
  35.8 27.0 reduce-scatter.2
  69.1 28.5 all-gather.1
  146.2 55.8 reduce-scatter.4
where the time goes:
time: 214 us; the launch traced here: 212 us
  waiting for transfers between devices  106 us (50%)
  local copies, waits for them, and re-layouts  37 us (17%)
  matrix products  25.1 us (12%)
  other arithmetic  24.4 us (11%)
  between operations  14.1 us (7%)
  starting transfers between devices  5.08 us (2%)
    reduce_scatter x1, waiting for transfers between devices, per_device(): lax.psum_scatter(summed * scale, 'tile', scatter_dimension=2, tiled=True)  46.2 us
    all_gather x1, waiting for transfers between devices, per_device(): resid_padded = lax.all_gather(share_padded, 'atom', axis=1, tiled=True)  28.4 us
    reduce_scatter x1, waiting for transfers between devices, per_device(): lax.psum_scatter(partial_value, 'atom', scatter_dimension=1, tiled=True)  27.1 us
    unnamed x35, local copies, waits for them, and re-layouts  17.6 us
    mul x1, other arithmetic, per_device(): summed * scale  17.3 us
    dot_general x4, matrix products, apply_band(): lax.dot_general(band, window, (((0,), (0,)), ((), ())), preferred_element...  17.1 us
    dot_general x2, matrix products, per_device(): lax.dot_general(window, rows, (((1,), (1,)), ((), ())), preferred_element...  8.03 us
    reshape x2, local copies, waits for them, and re-layouts, per_device(): dictionary.reshape(local_atoms, chans, TAP, TAP).transpose(2, 3, 0, 1)  5.04 us
  transfers between devices with their start and end apart: 7, of which 6 were waited for; matrix products, arithmetic and copies ran while one was open for 9% of the time, Pallas kernels for 0%

commit v1 on v0

--- a/solution.py
+++ b/solution.py
@@ -1,6 +1,8 @@
 import jax
 import jax.numpy as jnp
 from jax import lax
+from jax.experimental import pallas as pl
+from jax.experimental.pallas import tpu as pltpu
 from jax.sharding import PartitionSpec as P
 
 TAP = 9
@@ -10,6 +12,96 @@
 
 step_size = 0.1
 eps_sq = 0.01
+
+
+def greet(axis, count, me):
+    barrier = pltpu.get_barrier_semaphore()
+    for step in range(1, count):
+        pl.semaphore_signal(
+            barrier,
+            inc=1,
+            device_id={axis: lax.rem(me + step, count)},
+            device_id_type=pl.DeviceIdType.MESH,
+        )
+    pl.semaphore_wait(barrier, count - 1)
+
+
+def scatter_sum(blocks, axis, call_id):
+    count = blocks.shape[0]
+    piece = blocks.shape[1:]
+
+    def kernel(x_ref, o_ref, held, send_sem, recv_sem):
+        me = lax.axis_index(axis)
+        greet(axis, count, me)
+        copies = []
+        for step in range(1, count):
+            peer = lax.rem(me + step, count)
+            copy = pltpu.make_async_remote_copy(
+                src_ref=x_ref.at[peer],
+                dst_ref=held.at[step - 1],
+                send_sem=send_sem.at[step - 1],
+                recv_sem=recv_sem.at[step - 1],
+                device_id={axis: peer},
+                device_id_type=pl.DeviceIdType.MESH,
+            )
+            copy.start()
+            copies.append(copy)
+        for copy in copies:
+            copy.wait()
+        total = x_ref[me].astype(jnp.float32)
+        for step in range(1, count):
+            total += held[step - 1].astype(jnp.float32)
+        o_ref[...] = total
+
+    return pl.pallas_call(
+        kernel,
+        out_shape=jax.ShapeDtypeStruct(piece, jnp.float32),
+        in_specs=[pl.BlockSpec(memory_space=pltpu.VMEM)],
+        out_specs=pl.BlockSpec(memory_space=pltpu.VMEM),
+        scratch_shapes=[
+            pltpu.VMEM((count - 1,) + piece, blocks.dtype),
+            pltpu.SemaphoreType.DMA((count - 1,)),
+            pltpu.SemaphoreType.DMA((count - 1,)),
+        ],
+        compiler_params=pltpu.CompilerParams(collective_id=call_id, has_side_effects=True),
+    )(blocks)
+
+
+def gather(block, axis, call_id):
+    count = lax.axis_size(axis)
+
+    def kernel(x_ref, o_ref, held, send_sem, recv_sem):
+        me = lax.axis_index(axis)
+        greet(axis, count, me)
+        copies = []
+        for step in range(1, count):
+            copy = pltpu.make_async_remote_copy(
+                src_ref=x_ref,
+                dst_ref=held.at[step - 1],
+                send_sem=send_sem.at[step - 1],
+                recv_sem=recv_sem.at[step - 1],
+                device_id={axis: lax.rem(me + step, count)},
+                device_id_type=pl.DeviceIdType.MESH,
+            )
+            copy.start()
+            copies.append(copy)
+        o_ref[me] = x_ref[...]
+        for step, copy in enumerate(copies, 1):
+            copy.wait()
+            o_ref[lax.rem(me + count - step, count)] = held[step - 1]
+
+    return pl.pallas_call(
+        kernel,
+        out_shape=jax.ShapeDtypeStruct((count,) + block.shape, block.dtype),
+        in_specs=[pl.BlockSpec(memory_space=pltpu.VMEM)],
+        out_specs=pl.BlockSpec(memory_space=pltpu.VMEM),
+        scratch_shapes=[
+            pltpu.VMEM((count - 1,) + block.shape, block.dtype),
+            pltpu.SemaphoreType.DMA((count - 1,)),
+            pltpu.SemaphoreType.DMA((count - 1,)),
+        ],
+        compiler_params=pltpu.CompilerParams(collective_id=call_id, has_side_effects=True),
+    )(block)
 
 
 def rims(block):
@@ -64,13 +156,19 @@
     coef_cols = columns(jnp.concatenate([low * w_up, own, high * w_down], axis=0), width)
     taps = dictionary.reshape(local_atoms, chans, TAP, TAP).transpose(2, 3, 0, 1)
     partial_value = apply_band(coef_cols, banded(taps), strip_rows)
-    share = lax.psum_scatter(partial_value, "atom", scatter_dimension=1, tiled=True)
-    band_count = share.shape[1]
+    groups = lax.axis_size("atom")
+    band_count = chans // groups
+    pieces = partial_value.reshape(strip_rows, groups, band_count, width).transpose(1, 0, 2, 3)
+    share = scatter_sum(pieces.reshape(groups, -1, width), "atom", 0)
+    share = share.reshape(strip_rows, band_count, width)
     own_bands = lax.dynamic_slice_in_dim(image, lax.axis_index("atom") * band_count, band_count, 0)
     resid_share = (own_bands.transpose(1, 0, 2).astype(jnp.float32) - share).astype(jnp.bfloat16)
     low, high = rims(resid_share)
     share_padded = jnp.concatenate([low * w_up, resid_share, high * w_down], axis=0)
-    resid_padded = lax.all_gather(share_padded, "atom", axis=1, tiled=True)
+    padded_rows = share_padded.shape[0]
+    resid_all = gather(share_padded.reshape(-1, width), "atom", 1)
+    resid_all = resid_all.reshape(groups, padded_rows, band_count, width)
+    resid_padded = resid_all.transpose(1, 0, 2, 3).reshape(padded_rows, chans, width)
     residual = resid_padded[RIM : RIM + strip_rows].transpose(1, 0, 2)
     resid_cols = columns(resid_padded, width)
     flipped = taps[::-1, ::-1].transpose(0, 1, 3, 2)
@@ -86,8 +184,12 @@
         terms[j : j + TAP, :, :, j * local_atoms : (j + 1) * local_atoms] for j in range(BLOCK)
     )
     scale = 1.0 / jnp.sqrt(jnp.float32(strip_rows * strips * width))
-    part = lax.psum_scatter(summed * scale, "tile", scatter_dimension=2, tiled=True)
-    atom_step = part[::-1, ::-1].transpose(3, 2, 0, 1).reshape(local_atoms, -1)
+    half = chans // strips // 2
+    sides = (summed * scale).astype(jnp.bfloat16).reshape(-1, strips, 2, half, local_atoms)
+    packed = jnp.concatenate([sides[:, :, 0], sides[:, :, 1]], axis=-1).transpose(1, 0, 2, 3)
+    part = scatter_sum(packed.reshape(strips, -1, 2 * local_atoms), "tile", 2)
+    part = part.reshape(TAP, TAP, half, 2, local_atoms)[::-1, ::-1]
+    atom_step = part.transpose(4, 3, 2, 0, 1).reshape(local_atoms, -1)
 
     correlation = apply_band(resid_cols, banded(flipped), strip_rows).transpose(1, 0, 2)
     updated = coeffs.astype(jnp.float32) + step_size * correlation

time: 214 us -> 133 us (0.62)
  waiting for transfers between devices: 106 us -> 4.1 us
  Pallas kernels: 0 us -> 70 us
  other arithmetic: 24.4 us -> 9.28 us
  between operations: 14.1 us -> 1.03 us
  local copies, waits for them, and re-layouts: 37 us -> 26.2 us
  matrix products: 25.1 us -> 16.5 us
    reduce_scatter x2 -> x0, waiting for transfers between devices: 73.3 us -> none  [the longest x1 46.2 us: per_device(): lax.psum_scatter(summed * scale, 'tile', scatter_dimension=2, tiled=True)]
    pallas_call x0 -> x3, Pallas kernels: none -> 70 us  [the longest x2 42.1 us: scatter_sum(): pl.pallas_call(kernel, out_shape=jax.ShapeDtypeStruct(piece, jnp.float32)...]
    all_gather x1 -> x0, waiting for transfers between devices: 28.4 us -> none  [per_device(): resid_padded = lax.all_gather(share_padded, 'atom', axis=1, tiled=True)]
    mul x1 -> x0, other arithmetic: 17.3 us -> none  [per_device(): summed * scale]
    unnamed x35 -> x28, local copies, waits for them, and re-layouts: 17.6 us -> 11.6 us
    dot_general x4, matrix products: 17.1 us -> 11.9 us  [apply_band(): lax.dot_general(band, window, (((0,), (0,)), ((), ())), preferred_element...]
    dot_general x2, matrix products: 8.03 us -> 4.56 us  [per_device(): lax.dot_general(window, rows, (((1,), (1,)), ((), ())), preferred_element...]
    slice x1 -> x2, local copies, waits for them, and re-layouts: 4.39 us -> 1 us  [per_device(): residual = resid_padded[RIM:RIM + strip_rows].transpose(1, 0, 2)]
  transfers between devices with their start and end apart: 7 -> 4, of which waited for: 6 -> 3; matrix products, arithmetic and copies ran while one was open for 9% -> 7% of each run, Pallas kernels for 0% -> 0%
where the time goes in v1:
time: 133 us; the launch traced here: 132 us
  Pallas kernels  70 us (53%)
  local copies, waits for them, and re-layouts  26.2 us (20%)
  matrix products  16.5 us (12%)
  other arithmetic  9.28 us (7%)
  starting transfers between devices  5.07 us (4%)
  waiting for transfers between devices  4.1 us (3%)
    pallas_call x2, Pallas kernels, scatter_sum(): pl.pallas_call(kernel, out_shape=jax.ShapeDtypeStruct(piece, jnp.float32)...  42.1 us
    pallas_call x1, Pallas kernels, gather(): pl.pallas_call(kernel, out_shape=jax.ShapeDtypeStruct((count,) + block.sh...  27.9 us
    dot_general x4, matrix products, apply_band(): lax.dot_general(band, window, (((0,), (0,)), ((), ())), preferred_element...  11.9 us
    unnamed x28, local copies, waits for them, and re-layouts  11.6 us
    reshape x2, local copies, waits for them, and re-layouts, per_device(): dictionary.reshape(local_atoms, chans, TAP, TAP).transpose(2, 3, 0, 1)  5.01 us
    dot_general x2, matrix products, per_device(): lax.dot_general(window, rows, (((1,), (1,)), ((), ())), preferred_element...  4.56 us
    ppermute x2, waiting for transfers between devices, rims(): high = lax.ppermute(block[:RIM], 'tile', backward)  2.69 us
  transfers between devices with their start and end apart: 4, of which 3 were waited for; matrix products, arithmetic and copies ran while one was open for 7% of the time, Pallas kernels for 0%

profile of v1, /device:TPU:9, one launch (start us, length us, event | category | flops | bytes accessed | tf_op | source)
XLA Modules:
  0.0 132.1 jit_solution(8494017288736143641)
XLA Ops:
  0.6 1.2 copy.83
  1.9 1.3 collective-permute-start
  5.0 2.4 %copy.34 = bf16[64,5184]{0,1:T(8,128)(2,1)} copy(bf16[64,5184]{1,0:T(8,128)(2,1)} %param.7) | data formatting | bytes 1327104 | tf_op args[2]
  7.4 2.6 %reshape.87 = bf16[64,64,9,9]{0,3,2,1:T(8,128)(2,1)S(1)} reshape(bf16[64,5184]{0,1:T(8,128)(2,1)} %copy.34) | data formatting | bytes 1327104 | tf_op jit(solution)/shard_map/reshape | solution.py:157
  10.0 2.4 %copy.35 = bf16[64,64,9,9]{1,0,3,2:T(8,128)(2,1)} copy(bf16[64,64,9,9]{0,3,2,1:T(8,128)(2,1)S(1)} %reshape.87) | data formatting | bytes 1327104 | tf_op jit(solution)/shard_map/reshape | solution.py:157
  13.4 2.4 %collective-permute-done.1 = bf16[4,64,512]{2,1,0:T(8,128)(2,1)} collective-permute-done((bf16[4,64,512]{2,1,0:T(8,128)(2,1)S(1)}, bf16[4,64,512]{2,1,0:T(8,128)(2,1)}, u32[]{:S(2)}, u32[]{:S(2)}) %collective-permute-start.1) | collective-permute-done | bytes 262176 | tf_op jit(solution)/shard_map/ppermute | solution.py:112
  21.0 3.0 %fusion.27 = f32[256,512]{1,0:T(8,128)S(1)} fusion(bf16[16,9,64,512]{3,2,1,0:T(8,128)(2,1)S(1)} %fusion.45, bf16[9,9,64,64]{3,2,1,0:T(8,128)(2,1)S(1)} %bitcast.184), kind=kOutput, calls=%fused_computation.44 | convolution fusion | flops 1847328768 | bytes 8929280 | tf_op jit(solution)/shard_map/dot_general | solution.py:138
  24.0 3.0 %fusion.24 = f32[256,512]{1,0:T(8,128)S(1)} fusion(bf16[16,9,64,512]{3,2,1,0:T(8,128)(2,1)S(1)} %fusion.45, bf16[9,9,64,64]{3,2,1,0:T(8,128)(2,1)S(1)} %bitcast.185), kind=kOutput, calls=%fused_computation.43 | convolution fusion | flops 1847328768 | bytes 8929280 | tf_op jit(solution)/shard_map/dot_general | solution.py:138
  28.1 29.4 %shard_map.76 = f32[64,512]{1,0:T(8,128)} custom-call(f32[8,64,512]{2,1,0:T(8,128)} %bitcast.191), custom_call_target="tpu_custom_call" | custom-call | tf_op jit(solution)/shard_map/pallas_call | solution.py:56
  58.6 1.3 collective-permute-start.2
  59.9 1.4 %collective-permute-start.3 = (bf16[4,8,512]{2,0,1:T(4,128)(2,1)S(1)}, bf16[4,8,512]{2,0,1:T(4,128)(2,1)S(1)}, u32[]{:S(2)}, u32[]{:S(2)}) collective-permute-start(bf16[4,8,512]{2,0,1:T(4,128)(2,1)S(1)} %get-tuple-element.15), channel_id=1, source_target_pairs={{8,0},{16,8},{24,16},{0,24},{9,1},{17,9},{25,17},{1,25},{10,2},{18... | collective-permute-start | bytes 98312 | tf_op jit(solution)/shard_map/ppermute | solution.py:112
  61.3 1.4 %collective-permute-done.2 = bf16[4,8,512]{2,0,1:T(4,128)(2,1)S(1)} collective-permute-done((bf16[4,8,512]{2,0,1:T(4,128)(2,1)S(1)}, bf16[4,8,512]{2,0,1:T(4,128)(2,1)S(1)}, u32[]{:S(2)}, u32[]{:S(2)}) %collective-permute-start.2) | collective-permute-done | bytes 32800 | tf_op jit(solution)/shard_map/ppermute | solution.py:111
  63.9 27.9 %shard_map.77 = bf16[8,128,512]{2,1,0:T(8,128)(2,1)} custom-call(bf16[128,512]{1,0:T(8,128)(2,1)} %bitcast.195), custom_call_target="tpu_custom_call" | custom-call | tf_op jit(solution)/shard_map/pallas_call | solution.py:93
  91.8 1.4 %copy_bitcast_fusion.1 = bf16[16,64,512]{2,1,0:T(8,128)(2,1)S(1)} fusion(bf16[8,128,512]{2,1,0:T(8,128)(2,1)} %shard_map.77), kind=kLoop, calls=%fused_computation.101 | loop fusion | bytes 2097152 | tf_op jit(solution)/shard_map/reshape | solution.py:171
  97.3 3.0 %convolution_bitcast_fusion = f32[256,512]{1,0:T(8,128)} fusion(bf16[16,9,64,512]{3,2,1,0:T(8,128)(2,1)S(1)} %fusion.61, bf16[9,9,64,64]{2,3,1,0:T(8,128)(2,1)S(1)} %reverse_bitcast_fusion), kind=kOutput, calls=%fused_computation.41 | convolution fusion | flops 1847328768 | bytes 8929280 | tf_op jit(solution)/shard_map/dot_general | solution.py:138
  100.3 3.0 %convolution_bitcast_fusion.1 = f32[256,512]{1,0:T(8,128)} fusion(bf16[16,9,64,512]{3,2,1,0:T(8,128)(2,1)S(1)} %fusion.61, bf16[9,9,64,64]{2,3,1,0:T(8,128)(2,1)S(1)} %reverse_bitcast_fusion), kind=kOutput, calls=%fused_computation.42 | convolution fusion | flops 1847328768 | bytes 8929280 | tf_op jit(solution)/shard_map/dot_general | solution.py:138
  103.2 1.8 %fusion.69 = (bf16[12,9,64,512]{3,2,1,0:T(8,128)(2,1)S(1)}, bf16[12,9,64,512]{3,2,1,0:T(8,128)(2,1)S(1)}) fusion(bf16[16,9,64,512]{3,2,1,0:T(8,128)(2,1)S(1)} %fusion.61), kind=kLoop, calls=%fused_computation.119 | loop fusion | bytes 28311552 | tf_op jit(solution)/shard_map/slice | solution.py:130
  106.0 2.0 %fusion.72 = f32[6912,256]{1,0:T(8,128)S(1)} fusion(bf16[6912,512]{1,0:T(8,128)(2,1)S(1)} %bitcast.178, bf16[256,512]{1,0:T(8,128)(2,1)S(1)} %bitcast.193), kind=kOutput, calls=%fused_computation.122 | convolution fusion | flops 1811939328 | bytes 14417920 | tf_op jit(solution)/shard_map/dot_general | solution.py:179
  108.1 2.5 %convolution_add_fusion = f32[6912,256]{1,0:T(8,128)S(1)} fusion(f32[6912,256]{1,0:T(8,128)S(1)} %fusion.72, bf16[6912,512]{1,0:T(8,128)(2,1)S(1)} %bitcast.179, bf16[256,512]{1,0:T(8,128)(2,1)S(1)} %bitcast.192), kind=kOutput, calls=%fused_computation.16 | convolution fusion | flops 1813708800 | bytes 21495808 | tf_op jit(solution)/shard_map/dot_general | solution.py:179
  110.6 1.4 %fusion.23 = bf16[9,9,64,64]{3,2,1,0:T(8,128)(2,1)S(1)} fusion(f32[12,9,64,256]{3,2,1,0:T(8,128)S(1)} %bitcast.177), kind=kLoop, calls=%fused_computation.37 | loop fusion | flops 1658880 | bytes 5971968 | tf_op jit(solution)/shard_map/convert_element_type | solution.py:188
  112.3 1.2 copy_bitcast_fusion.2.x_ref
  113.5 12.7 %shard_map.78 = f32[648,128]{1,0:T(8,128)} custom-call(bf16[4,648,128]{2,1,0:T(8,128)(2,1)} %copy_bitcast_fusion.2.x_ref), custom_call_target="tpu_custom_call" | custom-call | tf_op jit(solution)/shard_map/pallas_call | solution.py:56
  126.2 1.4 %reshape.100 = f32[9,9,8,2,64]{4,3,2,1,0:T(2,128)S(1)} reshape(f32[648,128]{1,0:T(8,128)} %shard_map.78) | data formatting | bytes 663552 | tf_op jit(solution)/shard_map/reshape | solution.py:191
  130.7 1.5 %subtract_convert_fusion = bf16[64,8,512]{2,1,0:T(8,128)(2,1)} fusion(f32[8,64,512]{2,1,0:T(8,128)S(1)} %bitcast.189, bf16[64,8,512]{2,1,0:T(8,128)(2,1)S(1)} %copy-done.2, f32[64]{0:T(128)S(1)} %copy-done.4), kind=kLoop, calls=%fused_computation.100 | loop fusion | flops 2097152 | bytes 2097408 | tf_op jit(solution)/shard_map/convert_element_type | solution.py:198
  (54 shorter events, 19.7 us)
Async XLA Ops:
  1.9 10.6 %collective-permute-start = (bf16[4,64,512]{2,1,0:T(8,128)(2,1)S(1)}, bf16[4,64,512]{2,1,0:T(8,128)(2,1)}, u32[]{:S(2)}, u32[]{:S(2)}) collective-permute-start(bf16[4,64,512]{2,1,0:T(8,128)(2,1)S(1)} %get-tuple-element.12), channel_id=1, source_target_pairs={{0,8},{8,16},{16,24},{24,0},{1,9},{9,17},{17,25},{25,1},{2,10},{10... | collective-permute-start | bytes 786440 | tf_op jit(solution)/shard_map/ppermute | solution.py:111
  3.1 12.7 %collective-permute-start.1 = (bf16[4,64,512]{2,1,0:T(8,128)(2,1)S(1)}, bf16[4,64,512]{2,1,0:T(8,128)(2,1)}, u32[]{:S(2)}, u32[]{:S(2)}) collective-permute-start(bf16[4,64,512]{2,1,0:T(8,128)(2,1)S(1)} %get-tuple-element.13), channel_id=1, source_target_pairs={{8,0},{16,8},{24,16},{0,24},{9,1},{17,9},{25,17},{1,25},{10,2},{18... | collective-permute-start | bytes 786440 | tf_op jit(solution)/shard_map/ppermute | solution.py:112
  17.9 3.1 %copy-start.1 = (bf16[64,64,9,9]{1,0,3,2:T(8,128)(2,1)S(1)}, bf16[64,64,9,9]{1,0,3,2:T(8,128)(2,1)}, u32[]{:S(2)}) copy-start(bf16[64,64,9,9]{1,0,3,2:T(8,128)(2,1)} %copy.35) | copy-start | bytes 1990660
  58.6 4.1 %collective-permute-start.2 = (bf16[4,8,512]{2,0,1:T(4,128)(2,1)S(1)}, bf16[4,8,512]{2,0,1:T(4,128)(2,1)S(1)}, u32[]{:S(2)}, u32[]{:S(2)}) collective-permute-start(bf16[4,8,512]{2,0,1:T(4,128)(2,1)S(1)} %get-tuple-element.14), channel_id=1, source_target_pairs={{0,8},{8,16},{16,24},{24,0},{1,9},{9,17},{17,25},{25,1},{2,10},{10... | collective-permute-start | bytes 98312 | tf_op jit(solution)/shard_map/ppermute | solution.py:111
  59.9 3.1 %collective-permute-start.3 = (bf16[4,8,512]{2,0,1:T(4,128)(2,1)S(1)}, bf16[4,8,512]{2,0,1:T(4,128)(2,1)S(1)}, u32[]{:S(2)}, u32[]{:S(2)}) collective-permute-start(bf16[4,8,512]{2,0,1:T(4,128)(2,1)S(1)} %get-tuple-element.15), channel_id=1, source_target_pairs={{8,0},{16,8},{24,16},{0,24},{9,1},{17,9},{25,17},{1,25},{10,2},{18... | collective-permute-start | bytes 98312 | tf_op jit(solution)/shard_map/ppermute | solution.py:112
  91.8 3.5 %copy-start = (bf16[8,128,512]{2,1,0:T(8,128)(2,1)S(1)}, bf16[8,128,512]{2,1,0:T(8,128)(2,1)}, u32[]{:S(2)}) copy-start(bf16[8,128,512]{2,1,0:T(8,128)(2,1)} %shard_map.77) | copy-start | bytes 3145732
  112.0 17.5 %copy-start.3 = (f32[256,512]{1,0:T(8,128)S(1)}, f32[256,512]{1,0:T(8,128)}, u32[]{:S(2)}) copy-start(f32[256,512]{1,0:T(8,128)} %convolution_bitcast_fusion) | copy-start | bytes 1572868
  112.3 18.4 %copy-start.2 = (bf16[64,8,512]{2,1,0:T(8,128)(2,1)S(1)}, bf16[64,8,512]{2,1,0:T(8,128)(2,1)}, u32[]{:S(2)}) copy-start(bf16[64,8,512]{2,1,0:T(8,128)(2,1)} %param.6) | copy-start | bytes 1572868
  112.3 18.4 %copy-start.4 = (f32[64]{0:T(128)S(1)}, f32[64]{0:T(128)}, u32[]{:S(2)}) copy-start(f32[64]{0:T(128)} %param.8) | copy-start | bytes 772
